TPU v7x, 32 devices: a whole 2x2x4 slice. The times are simulated.
32 devices in a mesh: groups: 2 (over y), weight: 4 (over z), token: 2 (over x), sub: 2 (over core).
Axes of the slice: x: 2, y: 2, z: 4, core: 2. Of those that a mesh axis runs over, the one named last changes fastest.
Arguments:
- tokens: bfloat16 [512, 8192], P(('groups', 'token'), ('weight', 'sub')), parts along dimension 0, may hold values from -6 to 6
- gate_blocks: bfloat16 [2, 8, 384, 128, 128], P('token', ('weight', 'sub')), may hold values from -0.09375 to 0.09375
- up_blocks: bfloat16 [2, 8, 384, 128, 128], P('token', ('weight', 'sub')), may hold values from -0.09375 to 0.09375
- gate_list: int32 [2, 8, 384], P(None, ('weight', 'sub')), may hold values from 0 to 511, as said below
- gate_count: int32 [2, 8], P(None, ('weight', 'sub')), may hold values from 128 to 384, as said below
- up_list: int32 [2, 8, 384], P(None, ('weight', 'sub')), may hold values from 0 to 511, as said below
- up_count: int32 [2, 8], P(None, ('weight', 'sub')), may hold values from 128 to 384, as said below
- cotangent: bfloat16 [512, 16384], P(('groups', 'token'), ('weight', 'sub')), parts along dimension 0, may hold values from -0.375 to 0.375
Outputs:
- hidden: bfloat16 [512, 16384], P(('groups', 'token'), ('weight', 'sub')), parts along dimension 0
- gate_grad: bfloat16 [4, 8, 384, 128, 128], P(('groups', 'token'), ('weight', 'sub')), parts along dimension 0
- up_grad: bfloat16 [4, 8, 384, 128, 128], P(('groups', 'token'), ('weight', 'sub')), parts along dimension 0
There are 2 independent parts, one for each index of `groups`. A program takes and returns all parts, laid end to end along the dimension named above; an argument that names none is the same for every part. Nothing has to cross between parts.
Inputs may be any that keep to these rules, and one draw needn't show every extreme that they name: `gate_list`: the 384 entries of one owner are distinct block positions. `up_list`: the 384 entries of one owner are distinct block positions. The first gate_count[t, c] slots of owner (t, c) are live; some owner has exactly 384. The first up_count[t, c] slots of owner (t, c) are live; some owner has exactly 384.
All inputs are finite; a program needn't handle non-finite values.
Results may differ from a plain program's by a relative error of at most 0.0059.
Values may be sent and summed in bfloat16 or wider, within the bound.
A program may use at most 448 MiB of HBM per device.

v0:
```python
import jax
import jax.numpy as jnp
from jax import lax
from jax.sharding import PartitionSpec as P


def place_panel(blocks, slot_lists, slot_counts, row_blocks, col_blocks):
    owner_span, capacity, block_size, _ = blocks.shape
    live_slots = jnp.arange(capacity, dtype=jnp.int32)[None, :] < slot_counts[:, None]
    kept_blocks = jnp.where(live_slots[:, :, None, None], blocks, jnp.zeros_like(blocks))
    dense_panel = jnp.zeros(
        (owner_span, row_blocks, block_size, col_blocks, block_size), blocks.dtype
    )
    owner_index = jnp.arange(owner_span, dtype=jnp.int32)[:, None]
    dense_panel = dense_panel.at[
        owner_index, slot_lists // col_blocks, :, slot_lists % col_blocks, :
    ].set(kept_blocks)
    return dense_panel.reshape(owner_span * row_blocks * block_size, col_blocks * block_size)


def owner_products(features, delta, slot_lists, slot_counts, row_blocks, col_blocks, block_size):
    owners, capacity = slot_lists.shape
    full_term = jnp.dot(features.T, delta, preferred_element_type=jnp.float32)
    arranged = full_term.reshape(owners, row_blocks, block_size, col_blocks, block_size)
    owner_index = jnp.arange(owners, dtype=jnp.int32)[:, None]
    selected = arranged[owner_index, slot_lists // col_blocks, :, slot_lists % col_blocks, :]
    live_slots = jnp.arange(capacity, dtype=jnp.int32)[None, :] < slot_counts[:, None]
    selected = jnp.where(live_slots[:, :, None, None], selected, 0.0)
    return selected.astype(jnp.bfloat16)


def shards(tokens, gate_blocks, up_blocks, gate_list, gate_count, up_list, up_count, cotangent):
    owners = lax.axis_size("token")
    capacity = gate_blocks.shape[2]
    block_size = gate_blocks.shape[3]
    tok_rows = tokens.shape[0]
    panel_width = cotangent.shape[1]
    col_blocks = panel_width // block_size
    features = lax.all_gather(tokens, ("weight", "sub"), axis=1, tiled=True)
    row_blocks = features.shape[1] // block_size // owners
    slot_lists = (gate_list[:, 0, :], up_list[:, 0, :])
    slot_counts = (gate_count[:, 0], up_count[:, 0])
    zero_sums = jnp.zeros((tok_rows, panel_width), jnp.float32)
    running_sums = (zero_sums, zero_sums)
    pieces = (
        lax.all_gather(gate_blocks, "token", axis=0, tiled=True),
        lax.all_gather(up_blocks, "token", axis=0, tiled=True),
    )
    updated = []
    for running, owner_blocks, slot_list, slot_count in zip(
        running_sums, pieces, slot_lists, slot_counts
    ):
        dense_panel = place_panel(owner_blocks[:, 0], slot_list, slot_count, row_blocks, col_blocks)
        updated.append(jnp.dot(features, dense_panel, preferred_element_type=jnp.float32))
    gate_sum, up_sum = tuple(updated)
    sigmoid_gate = jax.nn.sigmoid(gate_sum)
    silu_gate = gate_sum * sigmoid_gate
    hidden = (silu_gate * up_sum).astype(jnp.bfloat16)
    cot_values = cotangent.astype(jnp.float32)
    gate_delta = (
        cot_values * up_sum * sigmoid_gate * (1.0 + gate_sum * (1.0 - sigmoid_gate))
    ).astype(jnp.bfloat16)
    up_delta = (cot_values * silu_gate).astype(jnp.bfloat16)
    gate_products = owner_products(
        features, gate_delta, slot_lists[0], slot_counts[0], row_blocks, col_blocks, block_size
    )
    up_products = owner_products(
        features, up_delta, slot_lists[1], slot_counts[1], row_blocks, col_blocks, block_size
    )
    gate_received, up_received = (
        lax.all_to_all(gate_products, "token", split_axis=0, concat_axis=0, tiled=True),
        lax.all_to_all(up_products, "token", split_axis=0, concat_axis=0, tiled=True),
    )
    gate_grad = jnp.sum(gate_received, axis=0, dtype=jnp.float32).astype(jnp.bfloat16)
    up_grad = jnp.sum(up_received, axis=0, dtype=jnp.float32).astype(jnp.bfloat16)
    gate_grad = gate_grad.reshape(1, 1, capacity, block_size, block_size)
    up_grad = up_grad.reshape(1, 1, capacity, block_size, block_size)
    return (hidden, gate_grad, up_grad)


def solution(mesh):
    return jax.shard_map(
        shards,
        mesh=mesh,
        in_specs=(
            P(("groups", "token"), ("weight", "sub")),
            P("token", ("weight", "sub"), None, None, None),
            P("token", ("weight", "sub"), None, None, None),
            P(None, ("weight", "sub"), None),
            P(None, ("weight", "sub")),
            P(None, ("weight", "sub"), None),
            P(None, ("weight", "sub")),
            P(("groups", "token"), ("weight", "sub")),
        ),
        out_specs=(
            P(("groups", "token"), ("weight", "sub")),
            P(("groups", "token"), ("weight", "sub"), None, None, None),
            P(("groups", "token"), ("weight", "sub"), None, None, None),
        ),
        check_vma=False,
    )
```

profile of v0, /device:TPU:0, one launch (start us, length us, event | category | flops | bytes accessed | tf_op | source)
XLA Modules:
  0.0 1326.2 jit_solution(15612383209441341759)
XLA Ops:
  7.2 0.0 copy-start.8
  7.2 0.0 copy-start.9
  7.2 0.0 copy-start.3
  7.2 0.0 copy-start.10
  7.2 0.0 copy-start.11
  7.2 0.0 all-gather.4.cloned.1.call-start
  7.3 0.7 all-gather.4.cloned.1.call-update
  8.0 0.0 all-gather.6.cloned.1.call-start
  8.0 0.7 all-gather.6.cloned.1.call-update
  8.7 0.0 all-gather.8.cloned.1.call-start
  8.7 0.7 all-gather.8.cloned.1.call-update
  9.4 0.0 copy-done.8
  9.5 0.0 copy-done.9
  9.6 0.6 fusion.30
  10.2 0.0 copy-done.3
  10.2 0.3 copy.25
  10.5 0.0 copy-start.1
  10.5 0.0 copy-done.10
  10.5 0.1 iota_compare_fusion.2
  10.6 0.0 copy-start.4
  10.6 0.0 copy-done.11
  10.6 0.1 iota_compare_fusion.1
  10.7 295.4 %all-gather.4.cloned.1.call-done = bf16[2,1,384,128,128]{4,3,2,1,0:T(8,128)(2,1)} async-done(((bf16[1,1,384,128,128]{4,3,2,1,0:T(8,128)(2,1)}), bf16[2,1,384,128,128]{4,3,2,1,0:T(8,128)(2,1)}) %all-gather.4.cloned.1.call-update) | async-done | bytes 25165840 | tf_op jit(solution)/shard_map/all_gather | solution.py:46
  306.0 21.2 %bitcast_select_fusion.1 = bf16[2,384,128,128]{3,2,1,0:T(8,128)(2,1)} fusion(bf16[2,1,384,128,128]{4,3,2,1,0:T(8,128)(2,1)} %all-gather.4.cloned.1.call-done, pred[2,384]{1,0:T(4,128)(4,1)S(1)} %iota_compare_fusion.2), kind=kLoop, calls=%fused_computation.15 | loop fusion | flops 12582912 | bytes 50332416 | tf_op jit(solution)/shard_map/jit(_where)/select_n | solution.py:10
  327.2 0.0 copy-done.4
  327.2 11.3 broadcast.265.clone
  338.5 130.5 %scatter_fusion = bf16[2,32,128,16,128]{4,2,3,1,0:T(8,128)(2,1)} fusion(bf16[2,32,128,16,128]{4,2,3,1,0:T(8,128)(2,1)} %broadcast.265.clone, s32[768]{0:T(1024)S(1)} %reshape.328, bf16[768,128,128]{2,1,0:T(8,128)(2,1)} %bitcast.84), kind=kCustom, calls=%fused_computation.2 | custom fusion | bytes 75506688 | tf_op jit(solution)/shard_map/scatter | solution.py:17
  469.0 34.6 %copy.23 = bf16[2,32,128,16,128]{4,3,2,1,0:T(8,128)(2,1)} copy(bf16[2,32,128,16,128]{4,2,3,1,0:T(8,128)(2,1)} %scatter_fusion) | data formatting | bytes 67108864 | tf_op jit(solution)/shard_map/scatter | solution.py:17
  503.6 0.0 all-gather.6.cloned.1.call-done
  503.6 0.0 copy-start
  503.6 16.6 %fusion.6 = f32[128,2048]{0,1:T(8,128)} fusion(bf16[128,8192]{1,0:T(8,128)(2,1)} %all-gather.6.cloned.1.call-done, bf16[1024,8,16,128]{3,2,1,0:T(8,128)(2,1)} %bitcast.86), kind=kOutput, calls=%fused_computation.16 | convolution fusion | flops 4294967296 | bytes 36700160 | tf_op jit(solution)/shard_map/dot_general | solution.py:54
  520.3 0.0 copy-done.1
  520.3 0.0 copy-done
  520.3 15.0 %convolution_bitcast_fusion = bf16[256,8,64,128]{3,1,2,0:T(8,128)(2,1)} fusion(bf16[128,8192]{1,0:T(8,128)(2,1)S(1)} %copy-done, bf16[128,2048]{0,1:T(8,128)(2,1)S(1)} %copy.25, f32[128,2048]{0,1:T(8,128)} %fusion.6), kind=kOutput, calls=%fused_computation.12 | convolution fusion | flops 4296802304 | bytes 37224448 | tf_op jit(solution)/shard_map/dot_general | solution.py:23
  535.3 23.0 %copy.32 = bf16[256,8,64,128]{3,2,1,0:T(8,128)(2,1)} copy(bf16[256,8,64,128]{3,1,2,0:T(8,128)(2,1)} %convolution_bitcast_fusion) | data formatting | bytes 67108864
  558.2 46.8 %copy.27 = bf16[2,32,128,16,128]{4,2,3,1,0:T(8,128)(2,1)} copy(bf16[2,32,128,16,128]{2,1,0,4,3:T(8,128)(2,1)} %bitcast.80) | data formatting | bytes 67108864 | tf_op jit(solution)/shard_map/reshape | solution.py:24
  605.0 32.6 %gather_fusion.1 = bf16[768,128,128]{2,1,0:T(8,128)(2,1)} fusion(bf16[2,32,128,16,128]{4,2,3,1,0:T(8,128)(2,1)} %copy.27, s32[768]{0:T(1024)S(1)} %reshape.322), kind=kCustom, calls=%fused_computation.1 | custom fusion | bytes 50340864 | tf_op jit(solution)/shard_map/gather | solution.py:26
  637.6 0.0 all-gather.8.cloned.1.call-done
  637.6 34.3 %select_convert_fusion = (bf16[2,384,128,128]{3,2,1,0:T(8,128)(2,1)}, bf16[2,384,128,128]{3,2,1,0:T(8,128)(2,1)}) fusion(bf16[2,384,128,128]{3,2,1,0:T(8,128)(2,1)} %bitcast.83, pred[2,384]{1,0:T(4,128)(4,1)S(1)} %iota_compare_fusion.1, bf16[2,1,384,128,128]{4,3,2,1,0:T(8,128)(2,1)} %all-gather.8.cloned.1.call-done), kind=kLoop, calls=%fused_computation.4 | loop fusion | flops 25165824 | bytes 100664064 | tf_op jit(solution)/shard_map/convert_element_type | solution.py:29
  672.0 0.0 copy-start.7
  672.0 0.0 copy-start.6
  672.0 11.8 all-to-all-start.1
  683.8 0.0 copy-done.7
  683.8 0.0 copy-done.6
  683.8 11.3 broadcast.265
  695.1 127.9 %scatter_fusion.1 = bf16[2,32,128,16,128]{4,2,3,1,0:T(8,128)(2,1)} fusion(bf16[2,32,128,16,128]{4,2,3,1,0:T(8,128)(2,1)} %broadcast.265, s32[768]{0:T(1024)S(1)} %reshape.334, bf16[768,128,128]{2,1,0:T(8,128)(2,1)} %bitcast.85), kind=kCustom, calls=%fused_computation.3 | custom fusion | bytes 75506688 | tf_op jit(solution)/shard_map/scatter | solution.py:17
  822.9 34.6 %copy.24 = bf16[2,32,128,16,128]{4,3,2,1,0:T(8,128)(2,1)} copy(bf16[2,32,128,16,128]{4,2,3,1,0:T(8,128)(2,1)} %scatter_fusion.1) | data formatting | bytes 67108864 | tf_op jit(solution)/shard_map/scatter | solution.py:17
  857.5 0.0 copy-start.2
  857.5 16.2 %multiply_convert_fusion = (bf16[128,2048]{0,1:T(8,128)(2,1)S(1)}, f32[128,2048]{0,1:T(8,128)}) fusion(f32[128,2048]{0,1:T(8,128)} %fusion.6, bf16[128,8192]{1,0:T(8,128)(2,1)S(1)} %copy-done, bf16[1024,8,16,128]{3,2,1,0:T(8,128)(2,1)} %bitcast.87), kind=kOutput, calls=%fused_computation.24 | convolution fusion | flops 4296540160 | bytes 38273024 | tf_op jit(solution)/shard_map/dot_general | solution.py:54
  873.7 0.0 copy-done.2
  873.7 15.3 %convolution_bitcast_fusion.1 = bf16[256,8,64,128]{3,1,2,0:T(8,128)(2,1)} fusion(bf16[128,8192]{1,0:T(8,128)(2,1)S(1)} %copy-done, f32[128,2048]{0,1:T(8,128)} %get-tuple-element.25, bf16[128,2048]{0,1:T(8,128)(2,1)S(1)} %copy-done.2, f32[128,2048]{0,1:T(8,128)} %fusion.6), kind=kOutput, calls=%fused_computation.13 | convolution fusion | flops 4297850880 | bytes 38273024 | tf_op jit(solution)/shard_map/dot_general | solution.py:23
  889.0 23.0 %copy.31 = bf16[256,8,64,128]{3,2,1,0:T(8,128)(2,1)} copy(bf16[256,8,64,128]{3,1,2,0:T(8,128)(2,1)} %convolution_bitcast_fusion.1) | data formatting | bytes 67108864
  912.0 46.8 %copy.26 = bf16[2,32,128,16,128]{4,2,3,1,0:T(8,128)(2,1)} copy(bf16[2,32,128,16,128]{2,1,0,4,3:T(8,128)(2,1)} %bitcast.81) | data formatting | bytes 67108864 | tf_op jit(solution)/shard_map/reshape | solution.py:24
  958.8 0.0 copy-start.5
  958.8 32.5 %gather_fusion = bf16[768,128,128]{2,1,0:T(8,128)(2,1)} fusion(bf16[2,32,128,16,128]{4,2,3,1,0:T(8,128)(2,1)} %copy.26, s32[768]{0:T(1024)S(1)} %reshape.316), kind=kCustom, calls=%fused_computation | custom fusion | bytes 50340864 | tf_op jit(solution)/shard_map/gather | solution.py:26
  991.3 0.0 copy-done.5
  991.3 22.4 %select_convert_fusion.1 = bf16[2,384,128,128]{3,2,1,0:T(8,128)(2,1)} fusion(bf16[2,384,128,128]{3,2,1,0:T(8,128)(2,1)} %bitcast.82, pred[2,384]{1,0:T(4,128)(4,1)S(1)} %copy-done.5), kind=kLoop, calls=%fused_computation.5 | loop fusion | flops 12582912 | bytes 50332416 | tf_op jit(solution)/shard_map/convert_element_type | solution.py:29
  1013.7 0.0 all-to-all-done.1
  1013.7 11.8 all-to-all-start
  1025.6 1.0 copy.28
  1026.6 21.9 %reduce_sum.25 = bf16[384,128,128]{2,1,0:T(8,128)(2,1)} reduce(bf16[2,384,128,128]{3,2,1,0:T(8,128)(2,1)} %all-to-all-done.1, bf16[]{:T(256)} %constant.56.clone.1), dimensions={0}, to_apply=%region_3.4 | reduce | flops 6291456 | bytes 37748736 | tf_op jit(solution)/shard_map/reduce_sum | solution.py:75
  1048.5 249.2 %all-to-all-done = bf16[2,384,128,128]{3,2,1,0:T(8,128)(2,1)} async-done(((bf16[2,384,128,128]{3,2,1,0:T(8,128)(2,1)}), bf16[2,384,128,128]{3,2,1,0:T(8,128)(2,1)}, u32[]{:S(2)}, u32[]{:S(2)}) %all-to-all-start) | async-done | bytes 25165856 | tf_op jit(solution)/shard_map/all_to_all | solution.py:71
  1297.7 21.7 %reduce_sum.24 = bf16[384,128,128]{2,1,0:T(8,128)(2,1)} reduce(bf16[2,384,128,128]{3,2,1,0:T(8,128)(2,1)} %all-to-all-done, bf16[]{:T(256)} %constant.56.clone.1), dimensions={0}, to_apply=%region_2.3 | reduce | flops 6291456 | bytes 37748736 | tf_op jit(solution)/shard_map/reduce_sum | solution.py:74
  (6 shorter events, 0.1 us)
Async XLA Ops:
  7.2 2.3 copy-start.8
  7.2 2.3 copy-start.9
  7.2 3.0 copy-start.3
  7.2 3.3 copy-start.10
  7.2 3.4 copy-start.11
  7.2 298.8 %all-gather.4.cloned.1.call-start = ((), (), s32[]{:S(2)}) async-start(), calls=%async_computation.2 | async-start | bytes 37748736 | tf_op jit(solution)/shard_map/all_gather | solution.py:46
  8.0 495.7 %all-gather.6.cloned.1.call-start = ((), (), s32[]{:S(2)}) async-start(), calls=%async_computation.3 | async-start | bytes 2359296 | tf_op jit(solution)/shard_map/all_gather | solution.py:39
  8.7 628.9 %all-gather.8.cloned.1.call-start = ((), (), s32[]{:S(2)}) async-start(), calls=%async_computation.4 | async-start | bytes 37748736 | tf_op jit(solution)/shard_map/all_gather | solution.py:47
  10.5 509.8 %copy-start.1 = (bf16[128,2048]{0,1:T(8,128)(2,1)}, bf16[128,2048]{0,1:T(8,128)(2,1)S(1)}, u32[]{:S(2)}) copy-start(bf16[128,2048]{0,1:T(8,128)(2,1)S(1)} %copy.25) | copy-start | bytes 1572868
  10.6 316.7 %copy-start.4 = (pred[2,384]{1,0:T(4,128)(4,1)}, pred[2,384]{1,0:T(4,128)(4,1)S(1)}, u32[]{:S(2)}) copy-start(pred[2,384]{1,0:T(4,128)(4,1)S(1)} %iota_compare_fusion.2) | copy-start | bytes 2308
  503.6 16.7 %copy-start = (bf16[128,8192]{1,0:T(8,128)(2,1)S(1)}, bf16[128,8192]{1,0:T(8,128)(2,1)}, u32[]{:S(2)}) copy-start(bf16[128,8192]{1,0:T(8,128)(2,1)} %all-gather.6.cloned.1.call-done) | copy-start | bytes 6291460
  672.0 11.8 copy-start.7
  672.0 11.8 copy-start.6
  672.0 341.7 %all-to-all-start.1 = ((bf16[2,384,128,128]{3,2,1,0:T(8,128)(2,1)}), bf16[2,384,128,128]{3,2,1,0:T(8,128)(2,1)}, u32[]{:S(2)}, u32[]{:S(2)}) async-start(bf16[2,384,128,128]{3,2,1,0:T(8,128)(2,1)} %get-tuple-element.22), calls=%async_computation.1 | async-start | bytes 50331648 | tf_op jit(solution)/shard_map/all_to_all | solution.py:72
  857.5 16.2 %copy-start.2 = (bf16[128,2048]{0,1:T(8,128)(2,1)S(1)}, bf16[128,2048]{0,1:T(8,128)(2,1)}, u32[]{:S(2)}) copy-start(bf16[128,2048]{0,1:T(8,128)(2,1)} %copy-done.1) | copy-start | bytes 1572868
  958.8 32.5 %copy-start.5 = (pred[2,384]{1,0:T(4,128)(4,1)S(1)}, pred[2,384]{1,0:T(4,128)(4,1)}, u32[]{:S(2)}) copy-start(pred[2,384]{1,0:T(4,128)(4,1)} %copy-done.4) | copy-start | bytes 2308
  1013.7 284.0 %all-to-all-start = ((bf16[2,384,128,128]{3,2,1,0:T(8,128)(2,1)}), bf16[2,384,128,128]{3,2,1,0:T(8,128)(2,1)}, u32[]{:S(2)}, u32[]{:S(2)}) async-start(bf16[2,384,128,128]{3,2,1,0:T(8,128)(2,1)} %select_convert_fusion.1), calls=%async_computation | async-start | bytes 50331648 | tf_op jit(solution)/shard_map/all_to_all | solution.py:71
Sparse Core Ops, SparseCore 0:
  9.6 296.3 all-gather.3
  307.6 29.0 all-gather.5
  338.3 293.1 all-gather.7
where the time goes:
time: 1350 us; the launch traced here: 1330 us
  local copies, waits for them, and re-layouts  556 us (41%)
  waiting for transfers between devices  547 us (41%)
  other arithmetic  122 us (9%)
  matrix products  63.2 us (5%)
  starting transfers between devices  23.7 us (2%)
  between operations  14.1 us (1%)
    scatter x4, local copies, waits for them, and re-layouts, place_panel(): dense_panel = dense_panel.at[owner_index, slot_lists // col_blocks, :, sl...  328 us
    all_gather x1, waiting for transfers between devices, shards(): lax.all_gather(gate_blocks, 'token', axis=0, tiled=True)  295 us
    all_to_all x1, waiting for transfers between devices, shards(): lax.all_to_all(gate_products, 'token', split_axis=0, concat_axis=0, tiled...  249 us
    reshape x2, local copies, waits for them, and re-layouts, owner_products(): full_term.reshape(owners, row_blocks, block_size, col_blocks, block_size)  93.6 us
    gather x2, local copies, waits for them, and re-layouts, owner_products(): arranged[owner_index, slot_lists // col_blocks, :, slot_lists % col_block...  65.2 us
    convert_element_type x2, other arithmetic, owner_products(): return selected.astype(jnp.bfloat16)  56.7 us
    unnamed x28, local copies, waits for them, and re-layouts  47.3 us
    dot_general x2, matrix products, shards(): jnp.dot(features, dense_panel, preferred_element_type=jnp.float32)  32.8 us
  transfers between devices with their start and end apart: 5, of which 2 were waited for; matrix products, arithmetic and copies ran while one was open for 52% of the time, Pallas kernels for 0%

commit v1 on v0

v1 whole, which is shorter than its diff:
```python
import functools

import jax
import jax.numpy as jnp
from jax import lax
from jax.experimental import pallas as pl
from jax.experimental.pallas import tpu as pltpu
from jax.sharding import PartitionSpec as P


def place_kernel(
    lists, counts, gate_blocks, up_blocks, placed, dense, blank, block_sems, out_sems
):
    capacity, block, _ = gate_blocks.shape
    depth, both = dense.shape
    width = both // 2
    cols = width // block
    strip = min(depth, 256)
    blank[...] = jnp.zeros_like(blank)
    sources = (gate_blocks, up_blocks)
    for m, source in enumerate(sources):

        @pl.loop(0, depth // strip)
        def _(i):
            rows = pl.ds(pl.multiple_of(i * strip, strip), strip)
            dense[rows, m * width : (m + 1) * width] = jnp.zeros((strip, width), dense.dtype)

        @pl.loop(0, capacity)
        def _(k):
            position = lists[m, k]
            row = pl.multiple_of(lax.div(position, cols) * block, block)
            col = pl.multiple_of(m * width + lax.rem(position, cols) * block, block)
            target = dense.at[pl.ds(row, block), pl.ds(col, block)]
            live = k < counts[m]

            @pl.when(live)
            def _():
                pltpu.make_async_copy(source.at[k], target, block_sems.at[m]).start()

            @pl.when(jnp.logical_not(live))
            def _():
                pltpu.make_async_copy(blank, target, block_sems.at[m]).start()

    writes = []
    for m, source in enumerate(sources):
        pltpu.make_async_copy(source, source, block_sems.at[m]).wait()
        half = pl.ds(m * width, width)
        write = pltpu.make_async_copy(dense.at[:, half], placed.at[:, half], out_sems.at[m])
        write.start()
        writes.append(write)
    for write in writes:
        write.wait()


def place(lists, counts, gate_blocks, up_blocks, depth, width):
    block = gate_blocks.shape[1]
    return pl.pallas_call(
        place_kernel,
        out_shape=jax.ShapeDtypeStruct((depth, 2 * width), gate_blocks.dtype),
        in_specs=[
            pl.BlockSpec(memory_space=pltpu.SMEM),
            pl.BlockSpec(memory_space=pltpu.SMEM),
            pl.BlockSpec(memory_space=pl.ANY),
            pl.BlockSpec(memory_space=pl.ANY),
        ],
        out_specs=pl.BlockSpec(memory_space=pl.ANY),
        scratch_shapes=[
            pltpu.VMEM((depth, 2 * width), gate_blocks.dtype),
            pltpu.VMEM((block, block), gate_blocks.dtype),
            pltpu.SemaphoreType.DMA((2,)),
            pltpu.SemaphoreType.DMA((2,)),
        ],
        compiler_params=pltpu.CompilerParams(vmem_limit_bytes=50 << 20),
        cost_estimate=pl.CostEstimate(
            flops=0, bytes_accessed=2 * gate_blocks.size * 2 + depth * width * 4, transcendentals=0
        ),
    )(lists, counts, gate_blocks, up_blocks)


def grad_kernel(lists, counts, turned, delta, gate_grad, up_grad, dense, sems):
    capacity, block, _ = gate_grad.shape
    depth = turned.shape[0]
    width = delta.shape[1] // 2
    cols = width // block
    strip = min(depth, 256)
    piece = min(width, 512)
    outs = (gate_grad, up_grad)
    for m, out in enumerate(outs):
        dense[m, depth : depth + block, 0:block] = jnp.zeros((block, block), dense.dtype)

        @pl.loop(0, depth // strip)
        def _(i):
            rows = pl.ds(pl.multiple_of(i * strip, strip), strip)
            for j in range(0, width, piece):
                dense[m, rows, j : j + piece] = jnp.dot(
                    turned[rows, :],
                    delta[:, m * width + j : m * width + j + piece],
                    preferred_element_type=jnp.float32,
                ).astype(dense.dtype)

        @pl.loop(0, capacity)
        def _(k):
            position = lists[m, k]
            live = k < counts[m]
            row = jnp.where(live, lax.div(position, cols) * block, depth)
            col = jnp.where(live, lax.rem(position, cols) * block, 0)
            source = dense.at[
                m, pl.ds(pl.multiple_of(row, block), block), pl.ds(pl.multiple_of(col, block), block)
            ]
            pltpu.make_async_copy(source, out.at[k], sems.at[m]).start()

    for m, out in enumerate(outs):
        pltpu.make_async_copy(out, out, sems.at[m]).wait()


def block_grads(lists, counts, turned, delta, capacity, block):
    depth = turned.shape[0]
    width = delta.shape[1] // 2
    shape = jax.ShapeDtypeStruct((capacity, block, block), jnp.bfloat16)
    return pl.pallas_call(
        grad_kernel,
        out_shape=(shape, shape),
        in_specs=[
            pl.BlockSpec(memory_space=pltpu.SMEM),
            pl.BlockSpec(memory_space=pltpu.SMEM),
            pl.BlockSpec(memory_space=pltpu.VMEM),
            pl.BlockSpec(memory_space=pltpu.VMEM),
        ],
        out_specs=(pl.BlockSpec(memory_space=pl.ANY), pl.BlockSpec(memory_space=pl.ANY)),
        scratch_shapes=[
            pltpu.VMEM((2, depth + block, width), jnp.bfloat16),
            pltpu.SemaphoreType.DMA((2,)),
        ],
        compiler_params=pltpu.CompilerParams(vmem_limit_bytes=56 << 20),
        cost_estimate=pl.CostEstimate(
            flops=4 * depth * width * turned.shape[1],
            bytes_accessed=4 * capacity * block * block,
            transcendentals=0,
        ),
    )(lists, counts, turned, delta)


def shards(tokens, gate_blocks, up_blocks, gate_list, gate_count, up_list, up_count, cotangent):
    owners = lax.axis_size("token")
    me = lax.axis_index("token")
    capacity, block = gate_blocks.shape[2:4]
    rows = tokens.shape[0]
    width = cotangent.shape[1]
    model = tokens.shape[1] * lax.axis_size("weight") * lax.axis_size("sub")
    depth = model // owners
    lists = jnp.stack([gate_list[me, 0], up_list[me, 0]])
    counts = jnp.stack([gate_count[me, 0], up_count[me, 0]])

    features = lax.all_gather(tokens, ("weight", "sub"), axis=1, tiled=True)
    placed = place(lists, counts, gate_blocks[0, 0], up_blocks[0, 0], depth, width)
    slices = lax.all_to_all(features, "token", split_axis=1, concat_axis=0, tiled=True)
    turned = slices.T

    partial = jnp.dot(slices, placed, preferred_element_type=jnp.float32)
    own = lax.dynamic_slice_in_dim(partial, me * rows, rows, axis=0)
    parts = lax.all_to_all(
        partial.astype(jnp.bfloat16), "token", split_axis=0, concat_axis=0, tiled=True
    ).reshape(owners, rows, 2 * width)
    sums = own
    for s in range(owners):
        sums = sums + jnp.where(me == s, 0.0, parts[s].astype(jnp.float32))
    gate, up = sums[:, :width], sums[:, width:]
    sigmoid = jax.nn.sigmoid(gate)
    silu = gate * sigmoid
    hidden = (silu * up).astype(jnp.bfloat16)
    cot = cotangent.astype(jnp.float32)
    gate_delta = (cot * up * sigmoid * (1.0 + gate * (1.0 - sigmoid))).astype(jnp.bfloat16)
    up_delta = (cot * silu).astype(jnp.bfloat16)
    delta = jnp.concatenate([gate_delta, up_delta], axis=1)
    delta = lax.all_gather(delta, "token", axis=0, tiled=True)
    gate_grad, up_grad = block_grads(lists, counts, turned, delta, capacity, block)
    shape = (1, 1, capacity, block, block)
    return (hidden, gate_grad.reshape(shape), up_grad.reshape(shape))


def solution(mesh):
    return jax.shard_map(
        shards,
        mesh=mesh,
        in_specs=(
            P(("groups", "token"), ("weight", "sub")),
            P("token", ("weight", "sub"), None, None, None),
            P("token", ("weight", "sub"), None, None, None),
            P(None, ("weight", "sub"), None),
            P(None, ("weight", "sub")),
            P(None, ("weight", "sub"), None),
            P(None, ("weight", "sub")),
            P(("groups", "token"), ("weight", "sub")),
        ),
        out_specs=(
            P(("groups", "token"), ("weight", "sub")),
            P(("groups", "token"), ("weight", "sub"), None, None, None),
            P(("groups", "token"), ("weight", "sub"), None, None, None),
        ),
        check_vma=False,
    )
```

time: 1350 us -> 200 us (0.15); the launches traced: 1330 us -> 200 us
  local copies, waits for them, and re-layouts: 556 us -> 6.21 us
  waiting for transfers between devices: 547 us -> 91.3 us
  other arithmetic: 122 us -> 6.51 us
  Pallas kernels: 0 us -> 54.6 us
  matrix products: 63.2 us -> 18.2 us
  starting transfers between devices: 23.7 us -> 8.81 us
    scatter x4 -> x0, local copies, waits for them, and re-layouts: 328 us -> none  [place_panel(): dense_panel = dense_panel.at[owner_index, slot_lists // col_blocks, :, sl...]
    all_gather x2 -> x1, waiting for transfers between devices: 295 us -> 30.7 us  [shards(): delta = lax.all_gather(delta, 'token', axis=0, tiled=True)]
    all_to_all x2, waiting for transfers between devices: 249 us -> 26.4 us  [the longest x1 26.4 us: shards(): lax.all_to_all(partial.astype(jnp.bfloat16), 'token', split_axis=0, conca...]
    reshape x2 -> x0, local copies, waits for them, and re-layouts: 93.6 us -> none  [owner_products(): full_term.reshape(owners, row_blocks, block_size, col_blocks, block_size)]
    gather x2 -> x0, local copies, waits for them, and re-layouts: 65.2 us -> none  [owner_products(): arranged[owner_index, slot_lists // col_blocks, :, slot_lists % col_block...]
    convert_element_type x2 -> x1, other arithmetic: 56.7 us -> 1.45 us  [shards(): (cot * up * sigmoid * (1.0 + gate * (1.0 - sigmoid))).astype(jnp.bfloat16)]
    pallas_call x0 -> x2, Pallas kernels: none -> 54.6 us  [the longest x1 27.9 us: place(): pl.pallas_call(place_kernel, out_shape=jax.ShapeDtypeStruct((depth, 2 * w...]
    unnamed x28 -> x14, local copies, waits for them, and re-layouts: 47.3 us -> 0.03 us
  transfers between devices with their start and end apart: 5 -> 4, of which waited for: 2 -> 3; matrix products, arithmetic and copies ran while one was open for 52% -> 2% of each run, Pallas kernels for 0% -> 14%
where the time goes in v1:
time: 200 us
  waiting for transfers between devices  91.3 us (46%)
  Pallas kernels  54.6 us (27%)
  matrix products  18.2 us (9%)
  between operations  14.2 us (7%)
  starting transfers between devices  8.81 us (4%)
  other arithmetic  6.51 us (3%)
  local copies, waits for them, and re-layouts  6.21 us (3%)
    all_gather x1, waiting for transfers between devices, shards(): features = lax.all_gather(tokens, ('weight', 'sub'), axis=1, tiled=True)  33.5 us
    all_gather x1, waiting for transfers between devices, shards(): delta = lax.all_gather(delta, 'token', axis=0, tiled=True)  30.7 us
    pallas_call x1, Pallas kernels, place(): pl.pallas_call(place_kernel, out_shape=jax.ShapeDtypeStruct((depth, 2 * w...  27.9 us
    pallas_call x1, Pallas kernels, block_grads(): pl.pallas_call(grad_kernel, out_shape=(shape, shape), in_specs=[pl.BlockS...  26.7 us
    all_to_all x1, waiting for transfers between devices, shards(): lax.all_to_all(partial.astype(jnp.bfloat16), 'token', split_axis=0, conca...  26.4 us
    dot_general x1, matrix products, shards(): partial = jnp.dot(slices, placed, preferred_element_type=jnp.float32)  18.2 us
    all_to_all x1, starting transfers between devices, shards(): lax.all_to_all(partial.astype(jnp.bfloat16), 'token', split_axis=0, conca...  4.82 us
    all_gather x1, local copies, waits for them, and re-layouts, shards(): features = lax.all_gather(tokens, ('weight', 'sub'), axis=1, tiled=True)  4.06 us
  transfers between devices with their start and end apart: 4, of which 3 were waited for; matrix products, arithmetic and copies ran while one was open for 2% of the time, Pallas kernels for 14%

profile of v1, /device:TPU:0, one launch (start us, length us, event | category | flops | bytes accessed | tf_op | source)
XLA Modules:
  0.0 199.8 jit_solution(4677108968317839062)
XLA Ops:
  7.2 0.0 all-gather.3.cloned.1.call-start
  7.2 0.7 all-gather.3.cloned.1.call-update
  7.9 33.5 %all-gather.3.cloned.1.call-done = bf16[128,8192]{1,0:T(8,128)(2,1)} async-done(((bf16[128,1024]{1,0:T(8,128)(2,1)}), bf16[128,8192]{1,0:T(8,128)(2,1)}) %all-gather.3.cloned.1.call-update) | async-done | bytes 2097168 | tf_op jit(solution)/shard_map/all_gather | solution.py:154
  41.4 4.1 %copy.12 = bf16[128,8192]{0,1:T(8,128)(2,1)} copy(bf16[128,8192]{1,0:T(8,128)(2,1)} %all-gather.3.cloned.1.call-done) | data formatting | bytes 4194304 | tf_op jit(solution)/shard_map/all_gather | solution.py:154
  45.5 0.0 copy-start.5
  45.5 0.0 copy-start.6
  45.5 0.0 copy-start.3
  45.5 0.0 copy-start.4
  45.5 3.9 %all-to-all-start = ((bf16[128,2,4096]{0,2,1:T(8,128)(2,1)}), bf16[128,2,4096]{0,2,1:T(8,128)(2,1)S(1)}, u32[]{:S(2)}, u32[]{:S(2)}) async-start(bf16[128,2,4096]{0,2,1:T(8,128)(2,1)} %bitcast.40), calls=%async_computation | async-start | bytes 4194304 | tf_op jit(solution)/shard_map/all_to_all | solution.py:156
  49.4 0.0 copy-done.5
  49.4 0.0 copy-done.6
  49.5 0.6 constant_dynamic-slice_fusion
  50.0 1.4 pad_add_fusion.1.counts
  51.4 0.0 copy-done.3
  51.4 0.0 copy-done.4
  51.4 0.0 copy-start.1
  51.4 0.0 copy-start
  51.4 27.9 %shard_map.103 = bf16[4096,4096]{1,0:T(8,128)(2,1)} custom-call(s32[2,384]{1,0:T(2,128)S(1)} %pad_add_fusion.lists, s32[2]{0:T(128)S(1)} %pad_add_fusion.1.counts, bf16[384,128,128]{2,1,0:T(8,128)(2,1)} %bitcast.38, bf16[384,128,128]{2,1,0:T(8,128)(2,1)} %bitcast.39), custom_call_target="tpu_custom_call" | custom-call | bytes 58720256 | tf_op jit(solution)/shard_map/pallas_call | solution.py:57
  79.3 0.0 copy-done.1
  79.4 0.0 copy-done
  79.4 0.0 all-to-all-done
  79.4 18.2 %fusion.8 = (bf16[4096,256]{0,1:T(8,128)(2,1)}, f32[4096,256]{0,1:T(8,128)}) fusion(bf16[4096,4096]{1,0:T(8,128)(2,1)} %shard_map.103, bf16[128,2,4096]{0,2,1:T(8,128)(2,1)S(1)} %all-to-all-done), kind=kOutput, calls=%fused_computation.22 | convolution fusion | flops 8590983168 | bytes 41943040 | tf_op jit(solution)/shard_map/dot_general | solution.py:159
  97.6 4.8 %all-to-all-start.1 = ((bf16[2,128,4096]{2,1,0:T(8,128)(2,1)}), bf16[2,128,4096]{2,1,0:T(8,128)(2,1)}, u32[]{:S(2)}, u32[]{:S(2)}) async-start(bf16[2,128,4096]{2,1,0:T(8,128)(2,1)} %bitcast.41), calls=%async_computation.1 | async-start | bytes 4194304 | tf_op jit(solution)/shard_map/all_to_all | solution.py:161
  102.4 0.0 all-gather.5.cloned.1.call-start
  102.5 26.4 %all-to-all-done.1 = bf16[2,128,4096]{2,1,0:T(8,128)(2,1)} async-done(((bf16[2,128,4096]{2,1,0:T(8,128)(2,1)}), bf16[2,128,4096]{2,1,0:T(8,128)(2,1)}, u32[]{:S(2)}, u32[]{:S(2)}) %all-to-all-start.1) | async-done | bytes 2097184 | tf_op jit(solution)/shard_map/all_to_all | solution.py:161
  128.8 0.0 copy-start.2
  128.8 2.6 %bitcast_add_fusion = f32[128,4096]{1,0:T(8,128)S(1)} fusion(f32[4096,256]{0,1:T(8,128)} %get-tuple-element.11, s32[]{:T(128)S(6)} %select_n.30, bf16[2,128,4096]{2,1,0:T(8,128)(2,1)} %all-to-all-done.1, pred[]{:T(512)S(6)} %eq.7, pred[]{:T(512)S(6)} %eq.6), kind=kLoop, calls=%fused_computation.3 | loop fusion | flops 3145728 | bytes 6291462 | tf_op jit(solution)/shard_map/add | solution.py:166
  131.5 0.0 copy-done.2
  131.5 1.4 fusion.5
  133.0 1.0 pad_maximum_fusion
  134.0 0.0 all-gather.5.cloned.1.call-update
  134.0 1.5 bitcast_bitcast_fusion.turned
  135.6 30.7 %all-gather.5.cloned.1.call-done.delta = bf16[256,4096]{1,0:T(8,128)(2,1)} async-done(((bf16[128,4096]{1,0:T(8,128)(2,1)}), bf16[256,4096]{1,0:T(8,128)(2,1)}) %all-gather.5.cloned.1.call-update) | async-done | bytes 2097168 | tf_op jit(solution)/shard_map/all_gather | solution.py:175
  166.2 26.7 %shard_map.104 = (bf16[384,128,128]{2,1,0:T(8,128)(2,1)}, bf16[384,128,128]{2,1,0:T(8,128)(2,1)}) custom-call(s32[2,384]{1,0:T(2,128)} %copy-done, s32[2]{0:T(128)} %copy-done.1, bf16[4096,256]{1,0:T(8,128)(2,1)} %bitcast_bitcast_fusion.turned, bf16[256,4096]{1,0:T(8,128)(2,1)} %all-gather.5.cloned.1.call-done.delta), custom_call_target="tpu_custom_call" | custom-call | flops 8589934592 | bytes 25165824 | tf_op jit(solution)/shard_map/pallas_call | solution.py:120
  (2 shorter events, 0.0 us)
Async XLA Ops:
  7.2 34.3 %all-gather.3.cloned.1.call-start = ((), (), s32[]{:S(2)}) async-start(), calls=%async_computation.2 | async-start | bytes 2359296 | tf_op jit(solution)/shard_map/all_gather | solution.py:154
  45.5 3.9 %copy-start.5 = (s32[2,1]{0,1:T(1,128)S(1)}, s32[2,1]{0,1:T(1,128)}, u32[]{:S(2)}) copy-start(s32[2,1]{0,1:T(1,128)} %param.14) | copy-start | bytes 28
  45.5 3.9 %copy-start.6 = (s32[2,1]{0,1:T(1,128)S(1)}, s32[2,1]{0,1:T(1,128)}, u32[]{:S(2)}) copy-start(s32[2,1]{0,1:T(1,128)} %param.12) | copy-start | bytes 28
  45.5 5.9 %copy-start.3 = (s32[2,1,384]{2,1,0:T(1,128)S(1)}, s32[2,1,384]{2,1,0:T(1,128)}, u32[]{:S(2)}) copy-start(s32[2,1,384]{2,1,0:T(1,128)} %param.13) | copy-start | bytes 9220
  45.5 5.9 %copy-start.4 = (s32[2,1,384]{2,1,0:T(1,128)S(1)}, s32[2,1,384]{2,1,0:T(1,128)}, u32[]{:S(2)}) copy-start(s32[2,1,384]{2,1,0:T(1,128)} %param.11) | copy-start | bytes 9220
  45.5 33.9 %all-to-all-start = ((bf16[128,2,4096]{0,2,1:T(8,128)(2,1)}), bf16[128,2,4096]{0,2,1:T(8,128)(2,1)S(1)}, u32[]{:S(2)}, u32[]{:S(2)}) async-start(bf16[128,2,4096]{0,2,1:T(8,128)(2,1)} %bitcast.40), calls=%async_computation | async-start | bytes 4194304 | tf_op jit(solution)/shard_map/all_to_all | solution.py:156
  51.4 27.9 %copy-start.1 = (s32[2]{0:T(128)}, s32[2]{0:T(128)S(1)}, u32[]{:S(2)}) copy-start(s32[2]{0:T(128)S(1)} %pad_add_fusion.1.counts) | copy-start | bytes 28
  51.4 27.9 %copy-start = (s32[2,384]{1,0:T(2,128)}, s32[2,384]{1,0:T(2,128)S(1)}, u32[]{:S(2)}) copy-start(s32[2,384]{1,0:T(2,128)S(1)} %pad_add_fusion.lists) | copy-start | bytes 9220
  97.6 31.2 %all-to-all-start.1 = ((bf16[2,128,4096]{2,1,0:T(8,128)(2,1)}), bf16[2,128,4096]{2,1,0:T(8,128)(2,1)}, u32[]{:S(2)}, u32[]{:S(2)}) async-start(bf16[2,128,4096]{2,1,0:T(8,128)(2,1)} %bitcast.41), calls=%async_computation.1 | async-start | bytes 4194304 | tf_op jit(solution)/shard_map/all_to_all | solution.py:161
  102.4 63.8 %all-gather.5.cloned.1.call-start = ((), (), s32[]{:S(2)}) async-start(), calls=%async_computation.3 | async-start | bytes 3145728 | tf_op jit(solution)/shard_map/all_gather | solution.py:175
  128.8 2.7 %copy-start.2 = (bf16[128,2048]{1,0:T(8,128)(2,1)S(1)}, bf16[128,2048]{1,0:T(8,128)(2,1)}, u32[]{:S(2)}) copy-start(bf16[128,2048]{1,0:T(8,128)(2,1)} %param.15) | copy-start | bytes 1572868
Sparse Core Ops, SparseCore 0:
  9.6 31.7 all-gather.2
  134.1 32.0 all-gather.4

commit v2 on v1

--- a/solution.py
+++ b/solution.py
@@ -1,11 +1,11 @@
-import functools
-
 import jax
 import jax.numpy as jnp
 from jax import lax
 from jax.experimental import pallas as pl
 from jax.experimental.pallas import tpu as pltpu
 from jax.sharding import PartitionSpec as P
+
+MESH = pl.DeviceIdType.MESH
 
 
 def place_kernel(
@@ -77,13 +77,228 @@
     )(lists, counts, gate_blocks, up_blocks)
 
 
+def exchange_kernel(
+    features, placed, cotangent, hidden, turned, delta,
+    weights, x_all, flipped, own, sent, landed, delta_all, hidden_all,
+    w_sems, x_send, x_recv, pass_send, pass_recv, p_send, p_recv, d_send, d_recv, out_sems,
+):
+    owners = lax.axis_size("token")
+    me = lax.axis_index("token")
+    sub = lax.axis_index("sub")
+    rows, depth = x_all.shape[1:]
+    chunks, _, pair = delta_all.shape
+    piece = pair // 2
+    width = chunks * piece
+    half = rows // 2
+    sibling = {"sub": 1 - sub}
+    ahead = [{"token": lax.rem(me + d, owners)} for d in range(owners)]
+    behind = [{"token": lax.rem(me + owners - d, owners)} for d in range(owners)]
+
+    barrier = pltpu.get_barrier_semaphore()
+    for d in range(1, owners):
+        pl.semaphore_signal(barrier, inc=1, device_id=ahead[d], device_id_type=MESH)
+    pl.semaphore_signal(barrier, inc=1, device_id=sibling, device_id_type=MESH)
+
+    def weight_copy(c, m):
+        cols = pl.ds(pl.multiple_of(m * width + c * piece, piece), piece)
+        return pltpu.make_async_copy(placed.at[:, cols], weights.at[:, cols], w_sems.at[c, m])
+
+    mine = pltpu.make_async_copy(
+        features.at[:, pl.ds(pl.multiple_of(me * depth, depth), depth)], x_all.at[0], out_sems.at[0]
+    )
+    mine.start()
+    for m in range(2):
+        weight_copy(0, m).start()
+    pl.semaphore_wait(barrier, owners)
+
+    share = pl.ds(pl.multiple_of(sub * half, half), half)
+    x_copies = []
+    for d in range(1, owners):
+        start = pl.multiple_of(lax.rem(me + d, owners) * depth, depth)
+        copy = pltpu.make_async_remote_copy(
+            src_ref=features.at[share, pl.ds(start, depth)],
+            dst_ref=x_all.at[d, share, :],
+            send_sem=x_send.at[d],
+            recv_sem=x_recv.at[d],
+            device_id=ahead[d],
+            device_id_type=MESH,
+        )
+        copy.start()
+        x_copies.append(copy)
+
+    @pl.loop(1, chunks)
+    def _(c):
+        for m in range(2):
+            weight_copy(c, m).start()
+
+    mine.wait()
+
+    def product(slot, c, m):
+        cols = pl.ds(pl.multiple_of(m * width + c * piece, piece), piece)
+        return jnp.dot(x_all[slot], weights[:, cols], preferred_element_type=jnp.float32)
+
+    @pl.loop(0, chunks)
+    def _(c):
+        for m in range(2):
+            weight_copy(c, m).wait()
+            own[c, :, m * piece : (m + 1) * piece] = product(0, c, m)
+
+    passes = []
+    for d in range(1, owners):
+        x_copies[d - 1].wait_recv()
+        copy = pltpu.make_async_remote_copy(
+            src_ref=x_all.at[d, share, :],
+            dst_ref=x_all.at[d, share, :],
+            send_sem=pass_send.at[d],
+            recv_sem=pass_recv.at[d],
+            device_id=sibling,
+            device_id_type=MESH,
+        )
+        copy.start()
+        passes.append(copy)
+
+    def part_copy(d, c):
+        return pltpu.make_async_remote_copy(
+            src_ref=sent.at[d - 1, c],
+            dst_ref=landed.at[d - 1, c],
+            send_sem=p_send.at[d, c],
+            recv_sem=p_recv.at[d, c],
+            device_id=behind[d],
+            device_id_type=MESH,
+        )
+
+    for d in range(1, owners):
+        passes[d - 1].wait_recv()
+
+        @pl.loop(0, chunks)
+        def _(c):
+            for m in range(2):
+                sent[d - 1, c, :, m * piece : (m + 1) * piece] = product(d, c, m).astype(sent.dtype)
+            part_copy(d, c).start()
+
+    tile = min(depth, 256)
+    for d in range(owners):
+
+        @pl.loop(0, depth // tile)
+        def _(i):
+            span = pl.ds(pl.multiple_of(i * tile, tile), tile)
+            flipped[span, d * rows : (d + 1) * rows] = x_all[d, :, span].T
+
+    turned_out = pltpu.make_async_copy(flipped, turned, out_sems.at[0])
+    turned_out.start()
+
+    def delta_copy(d, c):
+        return pltpu.make_async_remote_copy(
+            src_ref=delta_all.at[c, pl.ds(0, rows), :],
+            dst_ref=delta_all.at[c, pl.ds(d * rows, rows), :],
+            send_sem=d_send.at[d, c],
+            recv_sem=d_recv.at[d, c],
+            device_id=ahead[d],
+            device_id_type=MESH,
+        )
+
+    @pl.loop(0, chunks)
+    def _(c):
+        for d in range(1, owners):
+            part_copy(d, c).wait_recv()
+        cols = pl.ds(pl.multiple_of(c * piece, piece), piece)
+        gate = own[c, :, 0:piece]
+        up = own[c, :, piece:pair]
+        for d in range(1, owners):
+            gate = gate + landed[d - 1, c, :, 0:piece].astype(jnp.float32)
+            up = up + landed[d - 1, c, :, piece:pair].astype(jnp.float32)
+        sigmoid = jax.nn.sigmoid(gate)
+        silu = gate * sigmoid
+        hidden_all[:, cols] = (silu * up).astype(hidden_all.dtype)
+        cot = cotangent[:, cols].astype(jnp.float32)
+        gate_delta = cot * up * sigmoid * (1.0 + gate * (1.0 - sigmoid))
+        delta_all[c, 0:rows, 0:piece] = gate_delta.astype(delta_all.dtype)
+        delta_all[c, 0:rows, piece:pair] = (cot * silu).astype(delta_all.dtype)
+        for d in range(1, owners):
+            delta_copy(d, c).start()
+
+    hidden_out = pltpu.make_async_copy(hidden_all, hidden, out_sems.at[1])
+    hidden_out.start()
+
+    @pl.loop(0, chunks)
+    def _(c):
+        for d in range(1, owners):
+            delta_copy(d, c).wait_recv()
+        pltpu.make_async_copy(delta_all.at[c], delta.at[c], w_sems.at[c, 0]).start()
+
+    for copy in x_copies + passes:
+        copy.wait_send()
+
+    @pl.loop(0, chunks)
+    def _(c):
+        for d in range(1, owners):
+            part_copy(d, c).wait_send()
+            delta_copy(d, c).wait_send()
+        pltpu.make_async_copy(delta_all.at[c], delta.at[c], w_sems.at[c, 0]).wait()
+
+    turned_out.wait()
+    hidden_out.wait()
+
+
+def exchange(features, placed, cotangent, owners):
+    rows, width = cotangent.shape
+    depth = placed.shape[0]
+    piece = min(width, 512)
+    chunks = width // piece
+    everyone = owners * rows
+    dma = pltpu.SemaphoreType.DMA
+    return pl.pallas_call(
+        exchange_kernel,
+        out_shape=(
+            jax.ShapeDtypeStruct((rows, width), jnp.bfloat16),
+            jax.ShapeDtypeStruct((depth, everyone), jnp.bfloat16),
+            jax.ShapeDtypeStruct((chunks, everyone, 2 * piece), jnp.bfloat16),
+        ),
+        in_specs=[
+            pl.BlockSpec(memory_space=pl.ANY),
+            pl.BlockSpec(memory_space=pl.ANY),
+            pl.BlockSpec(memory_space=pltpu.VMEM),
+        ],
+        out_specs=(pl.BlockSpec(memory_space=pl.ANY),) * 3,
+        scratch_shapes=[
+            pltpu.VMEM((depth, 2 * width), jnp.bfloat16),
+            pltpu.VMEM((owners, rows, depth), jnp.bfloat16),
+            pltpu.VMEM((depth, everyone), jnp.bfloat16),
+            pltpu.VMEM((chunks, rows, 2 * piece), jnp.float32),
+            pltpu.VMEM((owners - 1, chunks, rows, 2 * piece), jnp.bfloat16),
+            pltpu.VMEM((owners - 1, chunks, rows, 2 * piece), jnp.bfloat16),
+            pltpu.VMEM((chunks, everyone, 2 * piece), jnp.bfloat16),
+            pltpu.VMEM((rows, width), jnp.bfloat16),
+            dma((chunks, 2)),
+            dma((owners,)),
+            dma((owners,)),
+            dma((owners,)),
+            dma((owners,)),
+            dma((owners, chunks)),
+            dma((owners, chunks)),
+            dma((owners, chunks)),
+            dma((owners, chunks)),
+            dma((2,)),
+        ],
+        compiler_params=pltpu.CompilerParams(
+            collective_id=0, has_side_effects=True, vmem_limit_bytes=56 << 20
+        ),
+        cost_estimate=pl.CostEstimate(
+            flops=4 * everyone * depth * width,
+            bytes_accessed=4 * depth * width,
+            transcendentals=rows * width,
+        ),
+    )(features, placed, cotangent)
+
+
 def grad_kernel(lists, counts, turned, delta, gate_grad, up_grad, dense, sems):
     capacity, block, _ = gate_grad.shape
     depth = turned.shape[0]
-    width = delta.shape[1] // 2
+    chunks, _, pair = delta.shape
+    piece = pair // 2
+    width = chunks * piece
     cols = width // block
     strip = min(depth, 256)
-    piece = min(width, 512)
     outs = (gate_grad, up_grad)
     for m, out in enumerate(outs):
         dense[m, depth : depth + block, 0:block] = jnp.zeros((block, block), dense.dtype)
@@ -91,10 +306,10 @@
         @pl.loop(0, depth // strip)
         def _(i):
             rows = pl.ds(pl.multiple_of(i * strip, strip), strip)
-            for j in range(0, width, piece):
-                dense[m, rows, j : j + piece] = jnp.dot(
+            for c in range(chunks):
+                dense[m, rows, c * piece : (c + 1) * piece] = jnp.dot(
                     turned[rows, :],
-                    delta[:, m * width + j : m * width + j + piece],
+                    delta[c, :, m * piece : (m + 1) * piece],
                     preferred_element_type=jnp.float32,
                 ).astype(dense.dtype)
 
@@ -115,7 +330,7 @@
 
 def block_grads(lists, counts, turned, delta, capacity, block):
     depth = turned.shape[0]
-    width = delta.shape[1] // 2
+    width = delta.shape[0] * delta.shape[2] // 2
     shape = jax.ShapeDtypeStruct((capacity, block, block), jnp.bfloat16)
     return pl.pallas_call(
         grad_kernel,
@@ -144,7 +359,6 @@
     owners = lax.axis_size("token")
     me = lax.axis_index("token")
     capacity, block = gate_blocks.shape[2:4]
-    rows = tokens.shape[0]
     width = cotangent.shape[1]
     model = tokens.shape[1] * lax.axis_size("weight") * lax.axis_size("sub")
     depth = model // owners
@@ -153,26 +367,7 @@
 
     features = lax.all_gather(tokens, ("weight", "sub"), axis=1, tiled=True)
     placed = place(lists, counts, gate_blocks[0, 0], up_blocks[0, 0], depth, width)
-    slices = lax.all_to_all(features, "token", split_axis=1, concat_axis=0, tiled=True)
-    turned = slices.T
-
-    partial = jnp.dot(slices, placed, preferred_element_type=jnp.float32)
-    own = lax.dynamic_slice_in_dim(partial, me * rows, rows, axis=0)
-    parts = lax.all_to_all(
-        partial.astype(jnp.bfloat16), "token", split_axis=0, concat_axis=0, tiled=True
-    ).reshape(owners, rows, 2 * width)
-    sums = own
-    for s in range(owners):
-        sums = sums + jnp.where(me == s, 0.0, parts[s].astype(jnp.float32))
-    gate, up = sums[:, :width], sums[:, width:]
-    sigmoid = jax.nn.sigmoid(gate)
-    silu = gate * sigmoid
-    hidden = (silu * up).astype(jnp.bfloat16)
-    cot = cotangent.astype(jnp.float32)
-    gate_delta = (cot * up * sigmoid * (1.0 + gate * (1.0 - sigmoid))).astype(jnp.bfloat16)
-    up_delta = (cot * silu).astype(jnp.bfloat16)
-    delta = jnp.concatenate([gate_delta, up_delta], axis=1)
-    delta = lax.all_gather(delta, "token", axis=0, tiled=True)
+    hidden, turned, delta = exchange(features, placed, cotangent, owners)
     gate_grad, up_grad = block_grads(lists, counts, turned, delta, capacity, block)
     shape = (1, 1, capacity, block, block)
     return (hidden, gate_grad.reshape(shape), up_grad.reshape(shape))

time: 200 us -> 142 us (0.71)
  waiting for transfers between devices: 91.3 us -> 2.01 us
  Pallas kernels: 54.6 us -> 122 us
  matrix products: 18.2 us -> 0 us
  starting transfers between devices: 8.81 us -> 0.04 us
  other arithmetic: 6.51 us -> 1.38 us
  local copies, waits for them, and re-layouts: 6.21 us -> 2.77 us
    pallas_call x0 -> x1, Pallas kernels: none -> 66.2 us  [exchange(): pl.pallas_call(exchange_kernel, out_shape=(jax.ShapeDtypeStruct((rows, wi...]
    all_gather x1, waiting for transfers between devices: 33.5 us -> 1.33 us  [shards(): features = lax.all_gather(tokens, ('weight', 'sub'), axis=1, tiled=True)]
    all_gather x1 -> x0, waiting for transfers between devices: 30.7 us -> none  [shards(): delta = lax.all_gather(delta, 'token', axis=0, tiled=True)]
    all_to_all x2 -> x0, waiting for transfers between devices: 26.4 us -> none  [the longest x1 26.4 us: shards(): lax.all_to_all(partial.astype(jnp.bfloat16), 'token', split_axis=0, conca...]
    dot_general x1 -> x0, matrix products: 18.2 us -> none  [shards(): partial = jnp.dot(slices, placed, preferred_element_type=jnp.float32)]
    all_to_all x2 -> x0, starting transfers between devices: 8.73 us -> none  [the longest x1 4.82 us: shards(): lax.all_to_all(partial.astype(jnp.bfloat16), 'token', split_axis=0, conca...]
    all_gather x1 -> x0, local copies, waits for them, and re-layouts: 4.06 us -> none  [shards(): features = lax.all_gather(tokens, ('weight', 'sub'), axis=1, tiled=True)]
    add x1 -> x0, other arithmetic: 2.65 us -> none  [shards(): sums = sums + jnp.where(me == s, 0.0, parts[s].astype(jnp.float32))]
  transfers between devices with their start and end apart: 4 -> 1, of which waited for: 3 -> 1; matrix products, arithmetic and copies ran while one was open for 2% -> 2% of each run, Pallas kernels for 14% -> 20%
where the time goes in v2:
time: 142 us
  Pallas kernels  122 us (86%)
  between operations  14.1 us (10%)
  local copies, waits for them, and re-layouts  2.77 us (2%)
  waiting for transfers between devices  2.01 us (1%)
    pallas_call x1, Pallas kernels, exchange(): pl.pallas_call(exchange_kernel, out_shape=(jax.ShapeDtypeStruct((rows, wi...  66.2 us
    pallas_call x1, Pallas kernels, place(): pl.pallas_call(place_kernel, out_shape=jax.ShapeDtypeStruct((depth, 2 * w...  28.8 us
    pallas_call x1, Pallas kernels, block_grads(): pl.pallas_call(grad_kernel, out_shape=(shape, shape), in_specs=[pl.BlockS...  26.7 us
  transfers between devices with their start and end apart: 1, of which 1 were waited for; matrix products, arithmetic and copies ran while one was open for 2% of the time, Pallas kernels for 20%

profile of v2, /device:TPU:0, one launch (start us, length us, event | category | flops | bytes accessed | tf_op | source)
XLA Modules:
  0.0 142.1 jit_solution(6336863138621310936)
XLA Ops:
  7.2 0.0 all-gather.2.cloned.1.call-start
  7.2 0.7 all-gather.2.cloned.1.call-update
  7.9 1.3 constant_dynamic-slice_fusion
  9.2 1.4 pad_add_fusion.1.counts
  10.5 0.0 copy-start.1
  10.5 0.7 dynamic-slice_bitcast_fusion
  11.2 0.0 copy-start
  11.3 28.8 %shard_map.103.placed = bf16[4096,4096]{1,0:T(8,128)(2,1)} custom-call(s32[2,384]{1,0:T(2,128)S(1)} %pad_add_fusion.lists, s32[2]{0:T(128)S(1)} %pad_add_fusion.1.counts, bf16[384,128,128]{2,1,0:T(8,128)(2,1)} %bitcast.10, bf16[384,128,128]{2,1,0:T(8,128)(2,1)} %bitcast.11), custom_call_target="tpu_custom_call" | custom-call | bytes 58720256 | tf_op jit(solution)/shard_map/pallas_call | solution.py:57
  40.1 0.0 copy-done.1
  40.1 0.0 copy-done
  40.1 1.3 all-gather.2.cloned.1.call-done.features
  41.4 66.2 %shard_map.104 = (bf16[128,2048]{1,0:T(8,128)(2,1)}, bf16[4096,256]{1,0:T(8,128)(2,1)}, bf16[4,256,1024]{2,1,0:T(8,128)(2,1)}) custom-call(bf16[128,8192]{1,0:T(8,128)(2,1)} %all-gather.2.cloned.1.call-done.features, bf16[4096,4096]{1,0:T(8,128)(2,1)} %shard_map.103.placed, bf16[128,2048]{1,0:T(8,128)(2,1)} %cotangent.1), custom_call_target="tpu_custom_call" | custom-call | flops 8589934592 | bytes 33554432 | tf_op jit(solution)/shard_map/pallas_call | solution.py:250
  107.7 0.0 copy-start.2
  107.7 26.7 %shard_map.105 = (bf16[384,128,128]{2,1,0:T(8,128)(2,1)}, bf16[384,128,128]{2,1,0:T(8,128)(2,1)}) custom-call(s32[2,384]{1,0:T(2,128)} %copy-done, s32[2]{0:T(128)} %copy-done.1, bf16[4096,256]{1,0:T(8,128)(2,1)} %get-tuple-element.9.turned, bf16[4,256,1024]{2,1,0:T(8,128)(2,1)} %get-tuple-element.10.delta), custom_call_target="tpu_custom_call" | custom-call | flops 8589934592 | bytes 25165824 | tf_op jit(solution)/shard_map/pallas_call | solution.py:335
  134.4 0.0 copy-done.2
  134.4 0.8 copy.12
  (1 shorter events, 0.0 us)
Async XLA Ops:
  7.2 34.3 %all-gather.2.cloned.1.call-start = ((), (), s32[]{:S(2)}) async-start(), calls=%async_computation | async-start | bytes 2359296 | tf_op jit(solution)/shard_map/all_gather | solution.py:368
  10.5 29.6 %copy-start.1 = (s32[2]{0:T(128)}, s32[2]{0:T(128)S(1)}, u32[]{:S(2)}) copy-start(s32[2]{0:T(128)S(1)} %pad_add_fusion.1.counts) | copy-start | bytes 28
  11.2 28.9 %copy-start = (s32[2,384]{1,0:T(2,128)}, s32[2,384]{1,0:T(2,128)S(1)}, u32[]{:S(2)}) copy-start(s32[2,384]{1,0:T(2,128)S(1)} %pad_add_fusion.lists) | copy-start | bytes 9220
  107.7 26.8 %copy-start.2 = (bf16[128,2048]{1,0:T(8,128)(2,1)S(1)}, bf16[128,2048]{1,0:T(8,128)(2,1)}, u32[]{:S(2)}) copy-start(bf16[128,2048]{1,0:T(8,128)(2,1)} %get-tuple-element.20) | copy-start | bytes 1572868
Sparse Core Ops, SparseCore 0:
  9.6 31.7 all-gather.1

commit v3 on v2

--- a/solution.py
+++ b/solution.py
@@ -9,41 +9,36 @@
 
 
 def place_kernel(
-    lists, counts, gate_blocks, up_blocks, placed, dense, blank, block_sems, out_sems
+    lists, counts, gate_blocks, up_blocks, placed, dense, held, block_sems, out_sems
 ):
     capacity, block, _ = gate_blocks.shape
     depth, both = dense.shape
     width = both // 2
     cols = width // block
     strip = min(depth, 256)
-    blank[...] = jnp.zeros_like(blank)
     sources = (gate_blocks, up_blocks)
+    reads, writes = [], []
     for m, source in enumerate(sources):
+        read = pltpu.make_async_copy(source, held.at[m], block_sems.at[m])
+        read.start()
+        reads.append(read)
+    for m in range(2):
 
         @pl.loop(0, depth // strip)
         def _(i):
             rows = pl.ds(pl.multiple_of(i * strip, strip), strip)
             dense[rows, m * width : (m + 1) * width] = jnp.zeros((strip, width), dense.dtype)
 
-        @pl.loop(0, capacity)
+        reads[m].wait()
+
+        @pl.loop(0, capacity, unroll=8)
         def _(k):
             position = lists[m, k]
             row = pl.multiple_of(lax.div(position, cols) * block, block)
             col = pl.multiple_of(m * width + lax.rem(position, cols) * block, block)
-            target = dense.at[pl.ds(row, block), pl.ds(col, block)]
-            live = k < counts[m]
-
-            @pl.when(live)
-            def _():
-                pltpu.make_async_copy(source.at[k], target, block_sems.at[m]).start()
-
-            @pl.when(jnp.logical_not(live))
-            def _():
-                pltpu.make_async_copy(blank, target, block_sems.at[m]).start()
-
-    writes = []
-    for m, source in enumerate(sources):
-        pltpu.make_async_copy(source, source, block_sems.at[m]).wait()
+            kept = jnp.where(k < counts[m], held[m, k], jnp.zeros((block, block), dense.dtype))
+            dense[pl.ds(row, block), pl.ds(col, block)] = kept
+
         half = pl.ds(m * width, width)
         write = pltpu.make_async_copy(dense.at[:, half], placed.at[:, half], out_sems.at[m])
         write.start()
@@ -53,7 +48,6 @@
 
 
 def place(lists, counts, gate_blocks, up_blocks, depth, width):
-    block = gate_blocks.shape[1]
     return pl.pallas_call(
         place_kernel,
         out_shape=jax.ShapeDtypeStruct((depth, 2 * width), gate_blocks.dtype),
@@ -66,11 +60,11 @@
         out_specs=pl.BlockSpec(memory_space=pl.ANY),
         scratch_shapes=[
             pltpu.VMEM((depth, 2 * width), gate_blocks.dtype),
-            pltpu.VMEM((block, block), gate_blocks.dtype),
+            pltpu.VMEM((2, *gate_blocks.shape), gate_blocks.dtype),
             pltpu.SemaphoreType.DMA((2,)),
             pltpu.SemaphoreType.DMA((2,)),
         ],
-        compiler_params=pltpu.CompilerParams(vmem_limit_bytes=50 << 20),
+        compiler_params=pltpu.CompilerParams(vmem_limit_bytes=60 << 20),
         cost_estimate=pl.CostEstimate(
             flops=0, bytes_accessed=2 * gate_blocks.size * 2 + depth * width * 4, transcendentals=0
         ),
@@ -80,7 +74,7 @@
 def exchange_kernel(
     features, placed, cotangent, hidden, turned, delta,
     weights, x_all, flipped, own, sent, landed, delta_all, hidden_all,
-    w_sems, x_send, x_recv, pass_send, pass_recv, p_send, p_recv, d_send, d_recv, out_sems,
+    w_sems, mine_sems, x_send, x_recv, pass_send, pass_recv, p_send, p_recv, d_send, d_recv, out_sems,
 ):
     owners = lax.axis_size("token")
     me = lax.axis_index("token")
@@ -89,7 +83,9 @@
     chunks, _, pair = delta_all.shape
     piece = pair // 2
     width = chunks * piece
-    half = rows // 2
+    local = features.shape[2]
+    subs = lax.axis_size("sub")
+    shares = depth // (local * subs)
     sibling = {"sub": 1 - sub}
     ahead = [{"token": lax.rem(me + d, owners)} for d in range(owners)]
     behind = [{"token": lax.rem(me + owners - d, owners)} for d in range(owners)]
@@ -103,35 +99,58 @@
         cols = pl.ds(pl.multiple_of(m * width + c * piece, piece), piece)
         return pltpu.make_async_copy(placed.at[:, cols], weights.at[:, cols], w_sems.at[c, m])
 
-    mine = pltpu.make_async_copy(
-        features.at[:, pl.ds(pl.multiple_of(me * depth, depth), depth)], x_all.at[0], out_sems.at[0]
-    )
-    mine.start()
+    def share(i):
+        return pl.ds(pl.multiple_of((i * subs + sub) * local, local), local)
+
+    mine = [
+        pltpu.make_async_copy(
+            features.at[me * shares + i], x_all.at[0, :, share(i)], mine_sems.at[i]
+        )
+        for i in range(shares)
+    ]
+    for copy in mine:
+        copy.start()
     for m in range(2):
         weight_copy(0, m).start()
     pl.semaphore_wait(barrier, owners)
 
-    share = pl.ds(pl.multiple_of(sub * half, half), half)
     x_copies = []
     for d in range(1, owners):
-        start = pl.multiple_of(lax.rem(me + d, owners) * depth, depth)
+        first = lax.rem(me + d, owners) * shares
+        for i in range(shares):
+            copy = pltpu.make_async_remote_copy(
+                src_ref=features.at[first + i],
+                dst_ref=x_all.at[d, :, share(i)],
+                send_sem=x_send.at[d, i],
+                recv_sem=x_recv.at[d, i],
+                device_id=ahead[d],
+                device_id_type=MESH,
+            )
+            copy.start()
+            x_copies.append(copy)
+
+    passes = []
+    for i in range(shares):
         copy = pltpu.make_async_remote_copy(
-            src_ref=features.at[share, pl.ds(start, depth)],
-            dst_ref=x_all.at[d, share, :],
-            send_sem=x_send.at[d],
-            recv_sem=x_recv.at[d],
-            device_id=ahead[d],
+            src_ref=features.at[me * shares + i],
+            dst_ref=x_all.at[0, :, share(i)],
+            send_sem=pass_send.at[0, i],
+            recv_sem=pass_recv.at[0, i],
+            device_id=sibling,
             device_id_type=MESH,
         )
         copy.start()
-        x_copies.append(copy)
+        passes.append(copy)
 
     @pl.loop(1, chunks)
     def _(c):
         for m in range(2):
             weight_copy(c, m).start()
 
-    mine.wait()
+    for copy in mine:
+        copy.wait()
+    for copy in passes:
+        copy.wait_recv()
 
     def product(slot, c, m):
         cols = pl.ds(pl.multiple_of(m * width + c * piece, piece), piece)
@@ -143,19 +162,19 @@
             weight_copy(c, m).wait()
             own[c, :, m * piece : (m + 1) * piece] = product(0, c, m)
 
-    passes = []
     for d in range(1, owners):
-        x_copies[d - 1].wait_recv()
-        copy = pltpu.make_async_remote_copy(
-            src_ref=x_all.at[d, share, :],
-            dst_ref=x_all.at[d, share, :],
-            send_sem=pass_send.at[d],
-            recv_sem=pass_recv.at[d],
-            device_id=sibling,
-            device_id_type=MESH,
-        )
-        copy.start()
-        passes.append(copy)
+        for i in range(shares):
+            x_copies[(d - 1) * shares + i].wait_recv()
+            copy = pltpu.make_async_remote_copy(
+                src_ref=x_all.at[d, :, share(i)],
+                dst_ref=x_all.at[d, :, share(i)],
+                send_sem=pass_send.at[d, i],
+                recv_sem=pass_recv.at[d, i],
+                device_id=sibling,
+                device_id_type=MESH,
+            )
+            copy.start()
+            passes.append(copy)
 
     def part_copy(d, c):
         return pltpu.make_async_remote_copy(
@@ -168,7 +187,8 @@
         )
 
     for d in range(1, owners):
-        passes[d - 1].wait_recv()
+        for i in range(shares):
+            passes[d * shares + i].wait_recv()
 
         @pl.loop(0, chunks)
         def _(c):
@@ -245,6 +265,7 @@
     depth = placed.shape[0]
     piece = min(width, 512)
     chunks = width // piece
+    shares = features.shape[0] // owners
     everyone = owners * rows
     dma = pltpu.SemaphoreType.DMA
     return pl.pallas_call(
@@ -270,10 +291,11 @@
             pltpu.VMEM((chunks, everyone, 2 * piece), jnp.bfloat16),
             pltpu.VMEM((rows, width), jnp.bfloat16),
             dma((chunks, 2)),
-            dma((owners,)),
-            dma((owners,)),
-            dma((owners,)),
-            dma((owners,)),
+            dma((shares,)),
+            dma((owners, shares)),
+            dma((owners, shares)),
+            dma((owners, shares)),
+            dma((owners, shares)),
             dma((owners, chunks)),
             dma((owners, chunks)),
             dma((owners, chunks)),
@@ -291,41 +313,51 @@
     )(features, placed, cotangent)
 
 
-def grad_kernel(lists, counts, turned, delta, gate_grad, up_grad, dense, sems):
+def grad_kernel(lists, counts, turned, delta, gate_grad, up_grad, dense, staged, sems):
     capacity, block, _ = gate_grad.shape
     depth = turned.shape[0]
     chunks, _, pair = delta.shape
     piece = pair // 2
     width = chunks * piece
     cols = width // block
-    strip = min(depth, 256)
+    positions = dense.shape[0] - 1
+    strip = min(depth, 512)
+    groups = sems.shape[1]
+    group = capacity // groups
     outs = (gate_grad, up_grad)
+    dense[positions] = jnp.zeros((block, block), dense.dtype)
+    writes = []
     for m, out in enumerate(outs):
-        dense[m, depth : depth + block, 0:block] = jnp.zeros((block, block), dense.dtype)
 
         @pl.loop(0, depth // strip)
         def _(i):
             rows = pl.ds(pl.multiple_of(i * strip, strip), strip)
             for c in range(chunks):
-                dense[m, rows, c * piece : (c + 1) * piece] = jnp.dot(
+                term = jnp.dot(
                     turned[rows, :],
                     delta[c, :, m * piece : (m + 1) * piece],
                     preferred_element_type=jnp.float32,
                 ).astype(dense.dtype)
-
-        @pl.loop(0, capacity)
-        def _(k):
-            position = lists[m, k]
-            live = k < counts[m]
-            row = jnp.where(live, lax.div(position, cols) * block, depth)
-            col = jnp.where(live, lax.rem(position, cols) * block, 0)
-            source = dense.at[
-                m, pl.ds(pl.multiple_of(row, block), block), pl.ds(pl.multiple_of(col, block), block)
-            ]
-            pltpu.make_async_copy(source, out.at[k], sems.at[m]).start()
-
-    for m, out in enumerate(outs):
-        pltpu.make_async_copy(out, out, sems.at[m]).wait()
+                for r in range(strip // block):
+                    for q in range(piece // block):
+                        place_at = (i * (strip // block) + r) * cols + c * (piece // block) + q
+                        dense[place_at] = term[
+                            r * block : (r + 1) * block, q * block : (q + 1) * block
+                        ]
+
+        for g in range(groups):
+
+            @pl.loop(0, group, unroll=8)
+            def _(j):
+                k = g * group + j
+                staged[m, k] = dense[jnp.where(k < counts[m], lists[m, k], positions)]
+
+            span = pl.ds(g * group, group)
+            write = pltpu.make_async_copy(staged.at[m, span], out.at[span], sems.at[m, g])
+            write.start()
+            writes.append(write)
+    for write in writes:
+        write.wait()
 
 
 def block_grads(lists, counts, turned, delta, capacity, block):
@@ -343,8 +375,9 @@
         ],
         out_specs=(pl.BlockSpec(memory_space=pl.ANY), pl.BlockSpec(memory_space=pl.ANY)),
         scratch_shapes=[
-            pltpu.VMEM((2, depth + block, width), jnp.bfloat16),
-            pltpu.SemaphoreType.DMA((2,)),
+            pltpu.VMEM((depth * width // block**2 + 1, block, block), jnp.bfloat16),
+            pltpu.VMEM((2, capacity, block, block), jnp.bfloat16),
+            pltpu.SemaphoreType.DMA((2, 4 if capacity % 32 == 0 else 1)),
         ],
         compiler_params=pltpu.CompilerParams(vmem_limit_bytes=56 << 20),
         cost_estimate=pl.CostEstimate(
@@ -365,7 +398,7 @@
     lists = jnp.stack([gate_list[me, 0], up_list[me, 0]])
     counts = jnp.stack([gate_count[me, 0], up_count[me, 0]])
 
-    features = lax.all_gather(tokens, ("weight", "sub"), axis=1, tiled=True)
+    features = lax.all_gather(tokens, "weight", axis=0)
     placed = place(lists, counts, gate_blocks[0, 0], up_blocks[0, 0], depth, width)
     hidden, turned, delta = exchange(features, placed, cotangent, owners)
     gate_grad, up_grad = block_grads(lists, counts, turned, delta, capacity, block)

time: 142 us -> 133 us (0.937)
  Pallas kernels: 122 us -> 107 us
  waiting for transfers between devices: 2.01 us -> 6.53 us
    pallas_call x1, Pallas kernels: 28.8 us -> 22 us  [place(): pl.pallas_call(place_kernel, out_shape=jax.ShapeDtypeStruct((depth, 2 * w...]
    pallas_call x1, Pallas kernels: 26.7 us -> 20.3 us  [block_grads(): pl.pallas_call(grad_kernel, out_shape=(shape, shape), in_specs=[pl.BlockS...]
    all_gather x1, waiting for transfers between devices: 1.33 us -> 5.85 us  [shards(): features = lax.all_gather(tokens, 'weight', axis=0)]
    pallas_call x1, Pallas kernels: 66.2 us -> 64.5 us  [exchange(): pl.pallas_call(exchange_kernel, out_shape=(jax.ShapeDtypeStruct((rows, wi...]
  transfers between devices with their start and end apart: 1 -> 1, of which waited for: 1 -> 1; matrix products, arithmetic and copies ran while one was open for 2% -> 3% of each run, Pallas kernels for 20% -> 17%
where the time goes in v3:
time: 133 us
  Pallas kernels  107 us (80%)
  between operations  14.1 us (11%)
  waiting for transfers between devices  6.53 us (5%)
  local copies, waits for them, and re-layouts  2.76 us (2%)
  other arithmetic  2.5 us (2%)
    pallas_call x1, Pallas kernels, exchange(): pl.pallas_call(exchange_kernel, out_shape=(jax.ShapeDtypeStruct((rows, wi...  64.5 us
    pallas_call x1, Pallas kernels, place(): pl.pallas_call(place_kernel, out_shape=jax.ShapeDtypeStruct((depth, 2 * w...  22 us
    pallas_call x1, Pallas kernels, block_grads(): pl.pallas_call(grad_kernel, out_shape=(shape, shape), in_specs=[pl.BlockS...  20.3 us
    all_gather x1, waiting for transfers between devices, shards(): features = lax.all_gather(tokens, 'weight', axis=0)  5.85 us
  transfers between devices with their start and end apart: 1, of which 1 were waited for; matrix products, arithmetic and copies ran while one was open for 3% of the time, Pallas kernels for 17%

profile of v3, /device:TPU:0, one launch (start us, length us, event | category | flops | bytes accessed | tf_op | source)
XLA Modules:
  0.0 132.7 jit_solution(6761226371919137317)
XLA Ops:
  7.2 0.0 all-gather.3.cloned.1.call-start
  7.2 0.7 all-gather.3.cloned.1.call-update
  7.9 1.3 constant_dynamic-slice_fusion
  9.2 1.9 %pad_add_fusion.1.counts = s32[2]{0:T(128)} fusion(s32[1]{0:T(128)} %bitcast.4, s32[1]{0:T(128)} %bitcast.3), kind=kLoop, calls=%fused_computation.5 | loop fusion | flops 2 | bytes 16 | tf_op jit(solution)/shard_map/stack | solution.py:399
  11.1 0.7 dynamic-slice_bitcast_fusion
  11.8 0.6 pad_add_fusion.lists
  12.4 22.0 %shard_map.103.placed = bf16[4096,4096]{1,0:T(8,128)(2,1)} custom-call(s32[2,384]{1,0:T(2,128)} %pad_add_fusion.lists, s32[2]{0:T(128)} %pad_add_fusion.1.counts, bf16[384,128,128]{2,1,0:T(8,128)(2,1)} %bitcast.11, bf16[384,128,128]{2,1,0:T(8,128)(2,1)} %bitcast.12), custom_call_target="tpu_custom_call" | custom-call | bytes 58720256 | tf_op jit(solution)/shard_map/pallas_call | solution.py:51
  34.4 5.9 %all-gather.3.cloned.1.call-done = bf16[512,1024]{1,0:T(8,128)(2,1)} async-done(((bf16[128,1024]{1,0:T(8,128)(2,1)}), bf16[512,1024]{1,0:T(8,128)(2,1)}) %all-gather.3.cloned.1.call-update) | async-done | bytes 1048592 | tf_op jit(solution)/shard_map/all_gather | solution.py:401
  40.2 64.5 %shard_map.104 = (bf16[128,2048]{1,0:T(8,128)(2,1)}, bf16[4096,256]{1,0:T(8,128)(2,1)}, bf16[4,256,1024]{2,1,0:T(8,128)(2,1)}) custom-call(bf16[4,128,1024]{2,1,0:T(8,128)(2,1)} %bitcast.13, bf16[4096,4096]{1,0:T(8,128)(2,1)} %shard_map.103.placed, bf16[128,2048]{1,0:T(8,128)(2,1)} %cotangent.1), custom_call_target="tpu_custom_call" | custom-call | flops 8589934592 | bytes 33554432 | tf_op jit(solution)/shard_map/pallas_call | solution.py:271
  104.8 0.0 copy-start
  104.8 20.3 %shard_map.105 = (bf16[384,128,128]{2,1,0:T(8,128)(2,1)}, bf16[384,128,128]{2,1,0:T(8,128)(2,1)}) custom-call(s32[2,384]{1,0:T(2,128)} %pad_add_fusion.lists, s32[2]{0:T(128)} %pad_add_fusion.1.counts, bf16[4096,256]{1,0:T(8,128)(2,1)} %get-tuple-element.9.turned, bf16[4,256,1024]{2,1,0:T(8,128)(2,1)} %get-tuple-element.10.delta), custom_call_target="tpu_custom_call" | custom-call | flops 8589934592 | bytes 25165824 | tf_op jit(solution)/shard_map/pallas_call | solution.py:367
  125.0 0.0 copy-done
  125.0 0.8 copy.12
Async XLA Ops:
  7.2 33.1 %all-gather.3.cloned.1.call-start = ((), (), s32[]{:S(2)}) async-start(), calls=%async_computation | async-start | bytes 1310720 | tf_op jit(solution)/shard_map/all_gather | solution.py:401
  104.8 20.3 %copy-start = (bf16[128,2048]{1,0:T(8,128)(2,1)S(1)}, bf16[128,2048]{1,0:T(8,128)(2,1)}, u32[]{:S(2)}) copy-start(bf16[128,2048]{1,0:T(8,128)(2,1)} %get-tuple-element.20) | copy-start | bytes 1572868
Sparse Core Ops, SparseCore 0:
  9.6 30.6 all-gather.2

commit v4 on v3

--- a/solution.py
+++ b/solution.py
@@ -74,7 +74,7 @@
 def exchange_kernel(
     features, placed, cotangent, hidden, turned, delta,
     weights, x_all, flipped, own, sent, landed, delta_all, hidden_all,
-    w_sems, mine_sems, x_send, x_recv, pass_send, pass_recv, p_send, p_recv, d_send, d_recv, out_sems,
+    w_sems, mine_sems, pass_send, pass_recv, p_send, p_recv, d_send, d_recv, out_sems,
 ):
     owners = lax.axis_size("token")
     me = lax.axis_index("token")
@@ -102,10 +102,13 @@
     def share(i):
         return pl.ds(pl.multiple_of((i * subs + sub) * local, local), local)
 
+    def held_share(d, i):
+        group = lax.rem(me + owners - d, owners)
+        return features.at[group * (shares * owners) + me * shares + i]
+
     mine = [
-        pltpu.make_async_copy(
-            features.at[me * shares + i], x_all.at[0, :, share(i)], mine_sems.at[i]
-        )
+        pltpu.make_async_copy(held_share(d, i), x_all.at[d, :, share(i)], mine_sems.at[d, i])
+        for d in range(owners)
         for i in range(shares)
     ]
     for copy in mine:
@@ -114,33 +117,20 @@
         weight_copy(0, m).start()
     pl.semaphore_wait(barrier, owners)
 
-    x_copies = []
-    for d in range(1, owners):
-        first = lax.rem(me + d, owners) * shares
-        for i in range(shares):
-            copy = pltpu.make_async_remote_copy(
-                src_ref=features.at[first + i],
-                dst_ref=x_all.at[d, :, share(i)],
-                send_sem=x_send.at[d, i],
-                recv_sem=x_recv.at[d, i],
-                device_id=ahead[d],
-                device_id_type=MESH,
-            )
-            copy.start()
-            x_copies.append(copy)
-
-    passes = []
-    for i in range(shares):
-        copy = pltpu.make_async_remote_copy(
-            src_ref=features.at[me * shares + i],
-            dst_ref=x_all.at[0, :, share(i)],
-            send_sem=pass_send.at[0, i],
-            recv_sem=pass_recv.at[0, i],
+    passes = [
+        pltpu.make_async_remote_copy(
+            src_ref=held_share(d, i),
+            dst_ref=x_all.at[d, :, share(i)],
+            send_sem=pass_send.at[d, i],
+            recv_sem=pass_recv.at[d, i],
             device_id=sibling,
             device_id_type=MESH,
         )
+        for d in range(owners)
+        for i in range(shares)
+    ]
+    for copy in passes:
         copy.start()
-        passes.append(copy)
 
     @pl.loop(1, chunks)
     def _(c):
@@ -155,26 +145,6 @@
     def product(slot, c, m):
         cols = pl.ds(pl.multiple_of(m * width + c * piece, piece), piece)
         return jnp.dot(x_all[slot], weights[:, cols], preferred_element_type=jnp.float32)
-
-    @pl.loop(0, chunks)
-    def _(c):
-        for m in range(2):
-            weight_copy(c, m).wait()
-            own[c, :, m * piece : (m + 1) * piece] = product(0, c, m)
-
-    for d in range(1, owners):
-        for i in range(shares):
-            x_copies[(d - 1) * shares + i].wait_recv()
-            copy = pltpu.make_async_remote_copy(
-                src_ref=x_all.at[d, :, share(i)],
-                dst_ref=x_all.at[d, :, share(i)],
-                send_sem=pass_send.at[d, i],
-                recv_sem=pass_recv.at[d, i],
-                device_id=sibling,
-                device_id_type=MESH,
-            )
-            copy.start()
-            passes.append(copy)
 
     def part_copy(d, c):
         return pltpu.make_async_remote_copy(
@@ -186,15 +156,16 @@
             device_id_type=MESH,
         )
 
-    for d in range(1, owners):
-        for i in range(shares):
-            passes[d * shares + i].wait_recv()
-
-        @pl.loop(0, chunks)
-        def _(c):
+    @pl.loop(0, chunks)
+    def _(c):
+        for m in range(2):
+            weight_copy(c, m).wait()
+        for d in range(1, owners):
             for m in range(2):
                 sent[d - 1, c, :, m * piece : (m + 1) * piece] = product(d, c, m).astype(sent.dtype)
             part_copy(d, c).start()
+        for m in range(2):
+            own[c, :, m * piece : (m + 1) * piece] = product(0, c, m)
 
     tile = min(depth, 256)
     for d in range(owners):
@@ -246,7 +217,7 @@
             delta_copy(d, c).wait_recv()
         pltpu.make_async_copy(delta_all.at[c], delta.at[c], w_sems.at[c, 0]).start()
 
-    for copy in x_copies + passes:
+    for copy in passes:
         copy.wait_send()
 
     @pl.loop(0, chunks)
@@ -265,7 +236,7 @@
     depth = placed.shape[0]
     piece = min(width, 512)
     chunks = width // piece
-    shares = features.shape[0] // owners
+    shares = features.shape[0] // owners**2
     everyone = owners * rows
     dma = pltpu.SemaphoreType.DMA
     return pl.pallas_call(
@@ -291,8 +262,6 @@
             pltpu.VMEM((chunks, everyone, 2 * piece), jnp.bfloat16),
             pltpu.VMEM((rows, width), jnp.bfloat16),
             dma((chunks, 2)),
-            dma((shares,)),
-            dma((owners, shares)),
             dma((owners, shares)),
             dma((owners, shares)),
             dma((owners, shares)),
@@ -398,7 +367,7 @@
     lists = jnp.stack([gate_list[me, 0], up_list[me, 0]])
     counts = jnp.stack([gate_count[me, 0], up_count[me, 0]])
 
-    features = lax.all_gather(tokens, "weight", axis=0)
+    features = lax.all_gather(tokens, ("token", "weight"), axis=0)
     placed = place(lists, counts, gate_blocks[0, 0], up_blocks[0, 0], depth, width)
     hidden, turned, delta = exchange(features, placed, cotangent, owners)
     gate_grad, up_grad = block_grads(lists, counts, turned, delta, capacity, block)

time: 133 us -> 145 us (1.090)
  waiting for transfers between devices: 6.53 us -> 28.4 us
  Pallas kernels: 107 us -> 96.5 us
    all_gather x1, waiting for transfers between devices: 5.85 us -> 27.7 us  [shards(): features = lax.all_gather(tokens, ('token', 'weight'), axis=0)]
    pallas_call x1, Pallas kernels: 64.5 us -> 54.3 us  [exchange(): pl.pallas_call(exchange_kernel, out_shape=(jax.ShapeDtypeStruct((rows, wi...]
  transfers between devices with their start and end apart: 1 -> 1, of which waited for: 1 -> 1; matrix products, arithmetic and copies ran while one was open for 3% -> 3% of each run, Pallas kernels for 17% -> 15%
where the time goes in v4:
time: 145 us; the launch traced here: 144 us
  Pallas kernels  96.5 us (67%)
  waiting for transfers between devices  28.4 us (20%)
  between operations  14.1 us (10%)
  local copies, waits for them, and re-layouts  2.76 us (2%)
  other arithmetic  2.54 us (2%)
    pallas_call x1, Pallas kernels, exchange(): pl.pallas_call(exchange_kernel, out_shape=(jax.ShapeDtypeStruct((rows, wi...  54.3 us
    all_gather x1, waiting for transfers between devices, shards(): features = lax.all_gather(tokens, ('token', 'weight'), axis=0)  27.7 us
    pallas_call x1, Pallas kernels, place(): pl.pallas_call(place_kernel, out_shape=jax.ShapeDtypeStruct((depth, 2 * w...  22 us
    pallas_call x1, Pallas kernels, block_grads(): pl.pallas_call(grad_kernel, out_shape=(shape, shape), in_specs=[pl.BlockS...  20.3 us
  transfers between devices with their start and end apart: 1, of which 1 were waited for; matrix products, arithmetic and copies ran while one was open for 3% of the time, Pallas kernels for 15%

profile of v4, /device:TPU:0, one launch (start us, length us, event | category | flops | bytes accessed | tf_op | source)
XLA Modules:
  0.0 144.3 jit_solution(1216155499014313220)
XLA Ops:
  7.2 0.0 all-gather.3.cloned.1.call-start
  7.2 0.7 all-gather.3.cloned.1.call-update
  7.9 1.3 constant_dynamic-slice_fusion
  9.2 2.0 %pad_add_fusion.1.counts = s32[2]{0:T(128)} fusion(s32[1]{0:T(128)} %bitcast.4, s32[1]{0:T(128)} %bitcast.3), kind=kLoop, calls=%fused_computation.5 | loop fusion | flops 2 | bytes 16 | tf_op jit(solution)/shard_map/stack | solution.py:368
  11.1 0.7 dynamic-slice_bitcast_fusion
  11.8 0.6 pad_add_fusion.lists
  12.4 22.0 %shard_map.103.placed = bf16[4096,4096]{1,0:T(8,128)(2,1)} custom-call(s32[2,384]{1,0:T(2,128)} %pad_add_fusion.lists, s32[2]{0:T(128)} %pad_add_fusion.1.counts, bf16[384,128,128]{2,1,0:T(8,128)(2,1)} %bitcast.11, bf16[384,128,128]{2,1,0:T(8,128)(2,1)} %bitcast.12), custom_call_target="tpu_custom_call" | custom-call | bytes 58720256 | tf_op jit(solution)/shard_map/pallas_call | solution.py:51
  34.4 27.7 %all-gather.3.cloned.1.call-done = bf16[1024,1024]{1,0:T(8,128)(2,1)} async-done(((bf16[128,1024]{1,0:T(8,128)(2,1)}), bf16[1024,1024]{1,0:T(8,128)(2,1)}) %all-gather.3.cloned.1.call-update) | async-done | bytes 2097168 | tf_op jit(solution)/shard_map/all_gather | solution.py:370
  62.1 54.3 %shard_map.104 = (bf16[128,2048]{1,0:T(8,128)(2,1)}, bf16[4096,256]{1,0:T(8,128)(2,1)}, bf16[4,256,1024]{2,1,0:T(8,128)(2,1)}) custom-call(bf16[8,128,1024]{2,1,0:T(8,128)(2,1)} %bitcast.13, bf16[4096,4096]{1,0:T(8,128)(2,1)} %shard_map.103.placed, bf16[128,2048]{1,0:T(8,128)(2,1)} %cotangent.1), custom_call_target="tpu_custom_call" | custom-call | flops 8589934592 | bytes 33554432 | tf_op jit(solution)/shard_map/pallas_call | solution.py:242
  116.4 0.0 copy-start
  116.4 20.3 %shard_map.105 = (bf16[384,128,128]{2,1,0:T(8,128)(2,1)}, bf16[384,128,128]{2,1,0:T(8,128)(2,1)}) custom-call(s32[2,384]{1,0:T(2,128)} %pad_add_fusion.lists, s32[2]{0:T(128)} %pad_add_fusion.1.counts, bf16[4096,256]{1,0:T(8,128)(2,1)} %get-tuple-element.9.turned, bf16[4,256,1024]{2,1,0:T(8,128)(2,1)} %get-tuple-element.10.delta), custom_call_target="tpu_custom_call" | custom-call | flops 8589934592 | bytes 25165824 | tf_op jit(solution)/shard_map/pallas_call | solution.py:336
  136.7 0.0 copy-done
  136.7 0.8 copy.12
Async XLA Ops:
  7.2 55.0 %all-gather.3.cloned.1.call-start = ((), (), s32[]{:S(2)}) async-start(), calls=%async_computation | async-start | bytes 2359296 | tf_op jit(solution)/shard_map/all_gather | solution.py:370
  116.4 20.3 %copy-start = (bf16[128,2048]{1,0:T(8,128)(2,1)S(1)}, bf16[128,2048]{1,0:T(8,128)(2,1)}, u32[]{:S(2)}) copy-start(bf16[128,2048]{1,0:T(8,128)(2,1)} %get-tuple-element.20) | copy-start | bytes 1572868
Sparse Core Ops, SparseCore 0:
  10.1 51.9 all-gather.2
